TPU v7x, 128 devices: a whole 4x4x4 slice. The times are simulated.
128 devices in a mesh: adapter: 32 (over y, x, core), mp: 4 (over z).
Axes of the slice: x: 4, y: 4, z: 4, core: 2. Of those that a mesh axis runs over, the one named last changes fastest.
Arguments:
- hidden: bfloat16 [8192, 4096], P('adapter', 'mp'), may hold values from -8 to 8
- subsets: int32 [8192, 8], P('adapter'), may hold values from 0 to 31, all different within a row; in each aligned block of 256 rows (0 to 255, 256 to 511, ...) at most 128 rows name the same one
- down_weight: bfloat16 [32, 4096, 256], P('adapter', 'mp'), may hold values from -0.09375 to 0.09375
- up_weight: bfloat16 [32, 256, 4096], P('adapter', None, 'mp'), may hold values from -0.375 to 0.375
- query_weight: bfloat16 [4096, 4096], P('mp'), may hold values from -0.08 to 2.08
- key_weight: bfloat16 [4096, 4096], P('mp'), may hold values from -0.08 to 2.08
Outputs:
- joined: bfloat16 [8192, 4096], P('adapter', 'mp')
Inputs may be any that keep to these rules, and one draw needn't show every extreme that they name: `subsets`: each row names 8 different adapters; within the rows of one index of the adapter axis no adapter is named by more than 128 rows.
All inputs are finite; a program needn't handle non-finite values.
Results may differ from a plain program's by a relative error of at most 0.025.
Values may be sent and summed in bfloat16 or wider, within the bound.
No kernel may reach another device: no remote copies, remote signals or barrier semaphores. Data moves between devices by JAX's collectives and lax.ppermute only.
A program may use at most 192 MiB of HBM per device.

v0:
```python
import jax
import jax.numpy as jnp
from jax import lax
from jax.sharding import PartitionSpec as P

D = 4096


def sent_to_all(x, axis):
    size = lax.axis_size(axis)
    return lax.all_to_all(jnp.broadcast_to(x[None], (size, *x.shape)), axis, 0, 0, tiled=True)


def over_copies(x, axis):
    return sent_to_all(x, axis).astype(jnp.float32).sum(axis=0)


def split_up(x, dim, size):
    before, after = (x.shape[:dim], x.shape[dim + 1 :])
    return jnp.moveaxis(x.reshape(*before, size, -1, *after), dim, 0)


def sent_and_summed(x, axis, dim):
    size = lax.axis_size(axis)
    parts = lax.all_to_all(split_up(x, dim, size), axis, 0, 0, tiled=True)
    return jnp.sum(parts.astype(jnp.float32), axis=0)


def in_order(parts, dim):
    parts = jnp.moveaxis(parts, 0, dim)
    shape = parts.shape
    return parts.reshape(*shape[:dim], shape[dim] * shape[dim + 1], *shape[dim + 2 :])


def collect(x, axis, dim):
    parts = sent_to_all(x, axis)
    return in_order(parts, dim)


def taken_together(x, axis):
    return sent_to_all(x, axis).sum(axis=0)


def tally(partial_sum):
    summed = over_copies(partial_sum.astype(jnp.bfloat16), "mp").astype(jnp.float32)
    return jnp.maximum(summed, 0.0).astype(jnp.bfloat16)


def per_device(hidden, subsets, down_weight, up_weight, query_weight, key_weight):
    row_count, width_local = hidden.shape
    fanout = subsets.shape[1]
    total_adapters = lax.axis_size("adapter") * down_weight.shape[0]
    capacity = min(row_count, 2 * row_count * fanout // total_adapters)
    labels = jnp.arange(total_adapters, dtype=jnp.int32)
    picks = (subsets[:, :, None] == labels[None, None, :]).astype(jnp.int32)
    chosen = jnp.sum(picks, axis=1)
    before = jnp.cumsum(chosen, axis=0) - chosen
    slot_rank = jnp.sum(picks * before[:, None, :], axis=2)
    flat_slot = subsets * capacity + slot_rank
    row_ids = jnp.broadcast_to(jnp.arange(row_count, dtype=jnp.int32)[:, None], flat_slot.shape)
    source_row = (
        jnp.zeros((total_adapters * capacity,), jnp.int32)
        .at[flat_slot.reshape(-1)]
        .set(row_ids.reshape(-1))
    )
    filled = jnp.zeros((total_adapters * capacity,), jnp.bool_).at[flat_slot.reshape(-1)].set(True)
    outgoing = jnp.where(
        filled[:, None], jnp.take(hidden, source_row, axis=0), jnp.zeros((), jnp.bfloat16)
    )
    outgoing = outgoing.reshape(total_adapters, capacity, width_local)
    query_part = jnp.dot(hidden, query_weight, preferred_element_type=jnp.float32)
    query_piece = sent_and_summed(query_part.astype(jnp.bfloat16), "mp", 1).astype(jnp.bfloat16)
    query = collect(query_piece, "mp", 1)
    probe = lax.dot_general(
        query, key_weight, (((1,), (1,)), ((), ())), preferred_element_type=jnp.float32
    ).astype(jnp.bfloat16)
    block = outgoing
    bottle = tally(
        jnp.einsum(
            "ncd,ndb->ncb",
            block,
            lax.all_gather(down_weight, "adapter", axis=0, tiled=True),
            preferred_element_type=jnp.float32,
        )
    )
    block = bottle
    returned = jnp.einsum(
        "ncb,nbd->ncd",
        block,
        lax.all_gather(up_weight, "adapter", axis=0, tiled=True),
        preferred_element_type=jnp.float32,
    ).astype(jnp.bfloat16)
    picked = jnp.take(returned.reshape(total_adapters * capacity, width_local), flat_slot, axis=0)
    widened = picked.astype(jnp.float32)
    base = hidden.astype(jnp.float32)
    probe_wide = probe.astype(jnp.float32)
    own_term = jnp.sum(base * probe_wide, axis=1)
    partial_logit = (
        jnp.einsum("rkd,rd->rk", widened, probe_wide, precision=lax.Precision.HIGHEST)
        + own_term[:, None]
    )
    logits = taken_together(partial_logit, "mp") * D ** (-0.5)
    share = jax.nn.softmax(logits, axis=-1)
    joined = base + jnp.einsum("rk,rkd->rd", share, widened, precision=lax.Precision.HIGHEST)
    return joined.astype(jnp.bfloat16)


def solution(mesh):
    return jax.shard_map(
        per_device,
        mesh=mesh,
        in_specs=(
            P("adapter", "mp"),
            P("adapter", None),
            P("adapter", "mp", None),
            P("adapter", None, "mp"),
            P("mp", None),
            P("mp", None),
        ),
        out_specs=P("adapter", "mp"),
        check_vma=False,
    )
```

profile of v0, /device:TPU:0, one launch (start us, length us, event | category | flops | bytes accessed | tf_op | source)
XLA Modules:
  0.0 257.7 jit_solution(9191249026218513655)
XLA Ops:
  6.5 0.7 all-gather.3.cloned.1.call-update
  7.3 0.7 all-gather.5.cloned.1.call-update
  8.0 5.9 %convolution_convert_fusion.1 = bf16[256,4096]{1,0:T(8,128)(2,1)S(1)} fusion(bf16[256,1024]{1,0:T(8,128)(2,1)} %param.6, bf16[1024,4096]{1,0:T(8,128)(2,1)} %param.10), kind=kOutput, calls=%fused_computation.11 | convolution fusion | flops 2148532224 | bytes 11010048 | tf_op jit(solution)/shard_map/dot_general | solution.py:71
  13.9 1.6 copy.58
  15.5 5.4 %all-to-all-start.1 = ((bf16[4,256,1024]{2,1,0:T(8,128)(2,1)}), bf16[4,256,1024]{2,1,0:T(8,128)(2,1)S(1)}, u32[]{:S(2)}, u32[]{:S(2)}) async-start(bf16[4,256,1024]{2,1,0:T(8,128)(2,1)} %bitcast.53), calls=%async_computation.1 | async-start | bytes 4194304 | tf_op jit(solution)/shard_map/all_to_all | solution.py:25
  21.0 0.6 reduce-window.6
  22.3 8.1 %scatter_custom_fusion.1 = s32[4096]{0:T(1024)S(1)} fusion(s32[2048]{0:T(1024)S(1)} %bitcast.55, s32[2048]{0:T(1024)S(1)} %reshape.120, s32[]{:T(128)} %constant.18.clone.1), kind=kCustom, calls=%fused_computation.45 | custom fusion | bytes 16388 | tf_op jit(solution)/shard_map/scatter | solution.py:64
  30.4 18.2 %gather_fusion = bf16[4096,1024]{1,0:T(8,128)(2,1)} fusion(bf16[256,1024]{1,0:T(8,128)(2,1)S(1)} %copy-done, s32[4096]{0:T(1024)S(1)} %fusion.19), kind=kCustom, calls=%fused_computation | custom fusion | bytes 16793600 | tf_op jit(solution)/shard_map/jit(_take)/gather | solution.py:68
  48.7 9.1 %scatter_custom_fusion = pred[4096]{0:T(1024)(128)(4,1)S(1)} fusion(s32[2048]{0:T(1024)S(1)} %bitcast.56, pred[2048]{0:T(1024)(128)(4,1)S(1)} %broadcast.50, pred[]{:T(512)} %constant.27.clone.1), kind=kCustom, calls=%fused_computation.48 | custom fusion | bytes 4097 | tf_op jit(solution)/shard_map/scatter | solution.py:66
  58.4 1.4 broadcast_in_dim.97
  59.9 4.8 %all-to-all-start.2 = ((bf16[4,256,1024]{1,2,0:T(8,128)(2,1)}), bf16[4,256,1024]{1,2,0:T(8,128)(2,1)}, u32[]{:S(2)}, u32[]{:S(2)}) async-start(bf16[4,256,1024]{1,2,0:T(8,128)(2,1)} %broadcast_in_dim.97), calls=%async_computation.2 | async-start | bytes 4194304 | tf_op jit(solution)/shard_map/all_to_all | solution.py:11
  64.7 19.8 %all-gather.3.cloned.1.call-done = bf16[32,1024,256]{2,1,0:T(8,128)(2,1)} async-done(((bf16[1,1024,256]{2,1,0:T(8,128)(2,1)}), bf16[32,1024,256]{2,1,0:T(8,128)(2,1)}) %all-gather.3.cloned.1.call-update) | async-done | bytes 16777232 | tf_op jit(solution)/shard_map/all_gather | solution.py:82
  84.5 9.7 %fusion.12 = bf16[32,128,256]{2,1,0:T(8,128)(2,1)S(1)} fusion(bf16[32,1024,256]{2,1,0:T(8,128)(2,1)} %all-gather.3.cloned.1.call-done, bf16[32,128,1024]{2,1,0:T(8,128)(2,1)} %bitcast.52, pred[32,128]{1,0:T(8,128)(4,1)S(1)} %and_bitcast_fusion, pred[32,128]{1,0:T(8,128)(4,1)S(1)} %bitcast.57), kind=kOutput, calls=%fused_computation.22 | convolution fusion | flops 2156920832 | bytes 27271168 | tf_op jit(solution)/shard_map/ncd,ndb->ncb/dot_general | solution.py:79
  94.2 4.3 %broadcast_in_dim.94 = bf16[4,32,128,256]{3,2,1,0:T(8,128)(2,1)} broadcast(bf16[32,128,256]{2,1,0:T(8,128)(2,1)S(1)} %fusion.12), dimensions={1,2,3} | broadcast | bytes 10485760 | tf_op jit(solution)/shard_map/broadcast_in_dim | solution.py:11
  98.4 5.8 %all-to-all-start = ((bf16[4,32,128,256]{3,2,1,0:T(8,128)(2,1)}), bf16[4,32,128,256]{3,2,1,0:T(8,128)(2,1)}, u32[]{:S(2)}, u32[]{:S(2)}) async-start(bf16[4,32,128,256]{3,2,1,0:T(8,128)(2,1)} %broadcast_in_dim.94), calls=%async_computation | async-start | bytes 16777216 | tf_op jit(solution)/shard_map/all_to_all | solution.py:11
  104.7 6.5 %fusion.15 = (f32[256]{0:T(256)S(1)}, bf16[256,1024]{1,0:T(8,128)(2,1)S(1)}) fusion(bf16[256,1024]{1,0:T(8,128)(2,1)S(1)} %copy-done, bf16[256,4096]{0,1:T(8,128)(2,1)} %bitcast.10, bf16[1024,4096]{1,0:T(8,128)(2,1)} %param.11), kind=kOutput, calls=%fused_computation.26 | convolution fusion | flops 2148794112 | bytes 11535360 | tf_op jit(solution)/shard_map/dot_general | solution.py:74
  111.3 87.5 %all-to-all-done = bf16[4,32,128,256]{3,2,1,0:T(8,128)(2,1)} async-done(((bf16[4,32,128,256]{3,2,1,0:T(8,128)(2,1)}), bf16[4,32,128,256]{3,2,1,0:T(8,128)(2,1)}, u32[]{:S(2)}, u32[]{:S(2)}) %all-to-all-start) | async-done | bytes 8388640 | tf_op jit(solution)/shard_map/all_to_all | solution.py:11
  198.8 4.9 %convert_reduce_fusion = bf16[32,128,256]{2,1,0:T(8,128)(2,1)S(1)} fusion(bf16[4,32,128,256]{3,2,1,0:T(8,128)(2,1)} %all-to-all-done), kind=kLoop, calls=%fused_computation.4 | loop fusion | flops 7340032 | bytes 10485760 | tf_op jit(solution)/shard_map/reduce_sum | solution.py:15
  203.8 11.4 %convolution_convert_fusion = bf16[32,128,1024]{2,1,0:T(8,128)(2,1)} fusion(bf16[32,256,1024]{2,1,0:T(8,128)(2,1)} %all-gather.5.cloned.1.call-done, bf16[32,128,256]{2,1,0:T(8,128)(2,1)S(1)} %convert_reduce_fusion), kind=kOutput, calls=%fused_computation.10 | convolution fusion | flops 2154823680 | bytes 27262976 | tf_op jit(solution)/shard_map/ncb,nbd->ncd/dot_general | solution.py:87
  215.1 15.4 %gather_fusion.1 = bf16[2048,1024]{1,0:T(8,128)(2,1)} fusion(bf16[4096,1024]{1,0:T(8,128)(2,1)} %bitcast.51, s32[2048]{0:T(1024)S(1)} %broadcast_clamp_fusion), kind=kCustom, calls=%fused_computation.1 | custom fusion | bytes 8396800 | tf_op jit(solution)/shard_map/jit(_take)/gather | solution.py:93
  230.6 5.3 %fusion.8 = f32[256,1,8]{2,1,0:T(1,128)S(1)} fusion(bf16[2048,1024]{1,0:T(8,128)(2,1)} %gather_fusion.1, pred[256,8]{1,0:T(8,128)(4,1)S(1)} %copy.38, bf16[256,1024,1]{1,0,2:T(8,128)(2,1)S(1)} %bitcast.58), kind=kOutput, calls=%fused_computation.17 | convolution fusion | flops 6291456 | bytes 4728832 | tf_op jit(solution)/shard_map/rkd,rd->rk/dot_general | solution.py:99
  236.0 7.8 %all_to_all.20 = f32[4,256,8]{1,2,0:T(8,128)S(1)} all-to-all(f32[4,256,8]{1,2,0:T(8,128)S(1)} %broadcast_in_dim.98), channel_id=1, replica_groups=mesh['adapter'=32,'mp'=4] {'mp'}, dimensions={0} | all-to-all | bytes 65536 | tf_op jit(solution)/shard_map/all_to_all | solution.py:11
  244.0 5.8 %fusion.7 = f32[256,1,1024]{2,1,0:T(1,128)S(1)} fusion(f32[256,8,1]{1,2,0:T(1,128)S(1)} %copy.46, bf16[2048,1024]{1,0:T(8,128)(2,1)} %gather_fusion.1, pred[256,8]{1,0:T(8,128)(4,1)S(1)} %copy.38), kind=kOutput, calls=%fused_computation.16 | convolution fusion | flops 27262976 | bytes 5253120 | tf_op jit(solution)/shard_map/rk,rkd->rd/dot_general | solution.py:104
  249.8 1.1 fusion.16
  (40 shorter events, 2.2 us)
Async XLA Ops:
  6.5 77.9 %all-gather.3.cloned.1.call-start = ((), (), s32[]{:S(2)}) async-start(), calls=%async_computation.4 | async-start | bytes 17301504 | tf_op jit(solution)/shard_map/all_gather | solution.py:82
  7.3 196.5 %all-gather.5.cloned.1.call-start = ((), (), s32[]{:S(2)}) async-start(), calls=%async_computation.5 | async-start | bytes 17301504 | tf_op jit(solution)/shard_map/all_gather | solution.py:90
  13.9 7.0 %copy-start.1 = (s32[256,8]{0,1:T(8,128)S(1)}, s32[256,8]{0,1:T(8,128)}, u32[]{:S(2)}) copy-start(s32[256,8]{0,1:T(8,128)} %param.7) | copy-start | bytes 24580
  13.9 16.5 %copy-start = (bf16[256,1024]{1,0:T(8,128)(2,1)S(1)}, bf16[256,1024]{1,0:T(8,128)(2,1)}, u32[]{:S(2)}) copy-start(bf16[256,1024]{1,0:T(8,128)(2,1)} %param.6) | copy-start | bytes 1572868
  15.5 42.3 %all-to-all-start.1 = ((bf16[4,256,1024]{2,1,0:T(8,128)(2,1)}), bf16[4,256,1024]{2,1,0:T(8,128)(2,1)S(1)}, u32[]{:S(2)}, u32[]{:S(2)}) async-start(bf16[4,256,1024]{2,1,0:T(8,128)(2,1)} %bitcast.53), calls=%async_computation.1 | async-start | bytes 4194304 | tf_op jit(solution)/shard_map/all_to_all | solution.py:25
  59.9 34.3 %all-to-all-start.2 = ((bf16[4,256,1024]{1,2,0:T(8,128)(2,1)}), bf16[4,256,1024]{1,2,0:T(8,128)(2,1)}, u32[]{:S(2)}, u32[]{:S(2)}) async-start(bf16[4,256,1024]{1,2,0:T(8,128)(2,1)} %broadcast_in_dim.97), calls=%async_computation.2 | async-start | bytes 4194304 | tf_op jit(solution)/shard_map/all_to_all | solution.py:11
  98.4 100.4 %all-to-all-start = ((bf16[4,32,128,256]{3,2,1,0:T(8,128)(2,1)}), bf16[4,32,128,256]{3,2,1,0:T(8,128)(2,1)}, u32[]{:S(2)}, u32[]{:S(2)}) async-start(bf16[4,32,128,256]{3,2,1,0:T(8,128)(2,1)} %broadcast_in_dim.94), calls=%async_computation | async-start | bytes 16777216 | tf_op jit(solution)/shard_map/all_to_all | solution.py:11
Sparse Core Ops, SparseCore 0:
  9.6 74.8 all-gather.2
  86.7 71.8 all-gather.4
where the time goes:
time: 258 us
  waiting for transfers between devices  109 us (42%)
  local copies, waits for them, and re-layouts  59.5 us (23%)
  matrix products  44.6 us (17%)
  starting transfers between devices  16.1 us (6%)
  between operations  13.6 us (5%)
  blocking collectives  7.81 us (3%)
  other arithmetic  7.31 us (3%)
    all_to_all x2, waiting for transfers between devices, sent_to_all(): lax.all_to_all(jnp.broadcast_to(x[None], (size, *x.shape)), axis, 0, 0, t...  87.5 us
    all_gather x1, waiting for transfers between devices, per_device(): lax.all_gather(down_weight, 'adapter', axis=0, tiled=True)  19.8 us
    gather x1, local copies, waits for them, and re-layouts, per_device(): jnp.take(hidden, source_row, axis=0)  18.2 us
    gather x1, local copies, waits for them, and re-layouts, per_device(): jnp.take(returned.reshape(total_adapters * capacity, width_local), flat_s...  15.4 us
    dot_general x1, matrix products, per_device(): jnp.einsum('ncb,nbd->ncd', block, lax.all_gather(up_weight, 'adapter', ax...  11.4 us
    all_to_all x2, starting transfers between devices, sent_to_all(): lax.all_to_all(jnp.broadcast_to(x[None], (size, *x.shape)), axis, 0, 0, t...  10.6 us
    dot_general x1, matrix products, per_device(): jnp.einsum('ncd,ndb->ncb', block, lax.all_gather(down_weight, 'adapter',...  9.7 us
    scatter x1, local copies, waits for them, and re-layouts, per_device(): jnp.zeros((total_adapters * capacity,), jnp.bool_).at[flat_slot.reshape(-1)]  9.12 us
  transfers between devices with their start and end apart: 5, of which 2 were waited for; matrix products, arithmetic and copies ran while one was open for 28% of the time, Pallas kernels for 0%

commit v1 on v0

--- a/solution.py
+++ b/solution.py
@@ -79,7 +79,12 @@
         jnp.einsum(
             "ncd,ndb->ncb",
             block,
-            lax.all_gather(down_weight, "adapter", axis=0, tiled=True),
+            jnp.concatenate(
+                lax.all_to_all(
+                    jnp.stack([down_weight] * lax.axis_size("adapter")), "adapter", 0, 0
+                ),
+                axis=0,
+            ),
             preferred_element_type=jnp.float32,
         )
     )

time: 258 us -> 479 us (1.86)
  the two profiles are of different devices: /device:TPU:0 before, /device:TPU:28 now
where the time goes in v1:
time: 479 us; the launch traced here: 478 us
  waiting for transfers between devices  291 us (61%)
  local copies, waits for them, and re-layouts  64.6 us (13%)
  matrix products  44.5 us (9%)
  blocking collectives  39.2 us (8%)
  starting transfers between devices  17.9 us (4%)
  between operations  13.7 us (3%)
  other arithmetic  7.31 us (2%)
    all_to_all x1, waiting for transfers between devices, per_device(): lax.all_to_all(jnp.stack([down_weight] * lax.axis_size('adapter')), 'adap...  187 us
    all_to_all x2, waiting for transfers between devices, sent_to_all(): lax.all_to_all(jnp.broadcast_to(x[None], (size, *x.shape)), axis, 0, 0, t...  103 us
    all_to_all x1, blocking collectives, sent_and_summed(): parts = lax.all_to_all(split_up(x, dim, size), axis, 0, 0, tiled=True)  31.4 us
    gather x1, local copies, waits for them, and re-layouts, per_device(): jnp.take(hidden, source_row, axis=0)  18.2 us
    gather x1, local copies, waits for them, and re-layouts, per_device(): jnp.take(returned.reshape(total_adapters * capacity, width_local), flat_s...  15.4 us
    dot_general x1, matrix products, per_device(): jnp.einsum('ncb,nbd->ncd', block, lax.all_gather(up_weight, 'adapter', ax...  11.4 us
    all_to_all x2, starting transfers between devices, sent_to_all(): lax.all_to_all(jnp.broadcast_to(x[None], (size, *x.shape)), axis, 0, 0, t...  10.3 us
    dot_general x1, matrix products, per_device(): jnp.einsum('ncd,ndb->ncb', block, jnp.concatenate(lax.all_to_all(jnp.stac...  9.72 us
  transfers between devices with their start and end apart: 4, of which 3 were waited for; matrix products, arithmetic and copies ran while one was open for 16% of the time, Pallas kernels for 0%

profile of v1, /device:TPU:28, one launch (start us, length us, event | category | flops | bytes accessed | tf_op | source)
XLA Modules:
  0.0 478.0 jit_solution(7472549547056646404)
XLA Ops:
  6.5 0.7 all-gather.2.cloned.1.call-update
  7.3 5.9 %convolution_convert_fusion.1 = bf16[256,4096]{1,0:T(8,128)(2,1)S(1)} fusion(bf16[256,1024]{1,0:T(8,128)(2,1)} %param.6, bf16[1024,4096]{1,0:T(8,128)(2,1)} %param.10), kind=kOutput, calls=%fused_computation.12 | convolution fusion | flops 2148532224 | bytes 11010048 | tf_op jit(solution)/shard_map/dot_general | solution.py:71
  13.4 31.4 %all_to_all.25 = bf16[4,256,1024]{2,1,0:T(8,128)(2,1)S(1)} all-to-all(bf16[4,256,1024]{2,1,0:T(8,128)(2,1)S(1)} %bitcast.58), channel_id=1, replica_groups=mesh['adapter'=32,'mp'=4] {'mp'}, dimensions={0} | all-to-all | bytes 4194304 | tf_op jit(solution)/shard_map/all_to_all | solution.py:25
  44.8 6.5 %stack.2 = bf16[32,1,1024,256]{3,2,1,0:T(8,128)(2,1)} broadcast(bf16[1024,256]{1,0:T(8,128)(2,1)S(1)} %bitcast.60), dimensions={2,3} | broadcast | bytes 17301504 | tf_op jit(solution)/shard_map/stack | solution.py:84
  51.3 7.6 %all-to-all-start = ((bf16[32,1,1024,256]{3,2,1,0:T(8,128)(2,1)}), bf16[32,1,1024,256]{3,2,1,0:T(8,128)(2,1)}, u32[]{:S(2)}, u32[]{:S(2)}) async-start(bf16[32,1,1024,256]{3,2,1,0:T(8,128)(2,1)} %stack.2), calls=%async_computation | async-start | bytes 33554432 | tf_op jit(solution)/shard_map/all_to_all | solution.py:83
  60.3 8.1 %scatter_custom_fusion.1 = s32[4096]{0:T(1024)S(1)} fusion(s32[2048]{0:T(1024)S(1)} %bitcast.61, s32[2048]{0:T(1024)S(1)} %reshape.127, s32[]{:T(128)} %constant.18.clone.1), kind=kCustom, calls=%fused_computation.46 | custom fusion | bytes 16388 | tf_op jit(solution)/shard_map/scatter | solution.py:64
  68.4 18.2 %gather_fusion = bf16[4096,1024]{1,0:T(8,128)(2,1)} fusion(bf16[256,1024]{1,0:T(8,128)(2,1)S(1)} %copy-done, s32[4096]{0:T(1024)S(1)} %fusion.22), kind=kCustom, calls=%fused_computation | custom fusion | bytes 16793600 | tf_op jit(solution)/shard_map/jit(_take)/gather | solution.py:68
  86.6 9.1 %scatter_custom_fusion = pred[4096]{0:T(1024)(128)(4,1)S(1)} fusion(s32[2048]{0:T(1024)S(1)} %bitcast.62, pred[2048]{0:T(1024)(128)(4,1)S(1)} %broadcast.53, pred[]{:T(512)} %constant.27.clone.1), kind=kCustom, calls=%fused_computation.49 | custom fusion | bytes 4097 | tf_op jit(solution)/shard_map/scatter | solution.py:66
  96.4 187.0 %all-to-all-done = bf16[32,1,1024,256]{3,2,1,0:T(8,128)(2,1)} async-done(((bf16[32,1,1024,256]{3,2,1,0:T(8,128)(2,1)}), bf16[32,1,1024,256]{3,2,1,0:T(8,128)(2,1)}, u32[]{:S(2)}, u32[]{:S(2)}) %all-to-all-start) | async-done | bytes 16777248 | tf_op jit(solution)/shard_map/all_to_all | solution.py:83
  283.4 1.5 broadcast_in_dim.97
  284.9 4.6 all-to-all-start.3
  289.5 9.7 %fusion.13 = bf16[32,128,256]{2,1,0:T(8,128)(2,1)S(1)} fusion(bf16[32,1,1024,256]{3,2,1,0:T(8,128)(2,1)} %all-to-all-done, bf16[32,128,1024]{2,1,0:T(8,128)(2,1)} %bitcast.57, pred[32,128]{1,0:T(8,128)(4,1)S(1)} %and_bitcast_fusion, pred[32,128]{1,0:T(8,128)(4,1)S(1)} %bitcast.63), kind=kOutput, calls=%fused_computation.23 | convolution fusion | flops 2156920832 | bytes 27271168 | tf_op jit(solution)/shard_map/ncd,ndb->ncb/dot_general | solution.py:79
  299.2 17.1 %all-to-all-done.3 = bf16[4,256,1024]{1,2,0:T(8,128)(2,1)} async-done(((bf16[4,256,1024]{1,2,0:T(8,128)(2,1)}), bf16[4,256,1024]{1,2,0:T(8,128)(2,1)}, u32[]{:S(2)}, u32[]{:S(2)}) %all-to-all-start.3) | async-done | bytes 2097184 | tf_op jit(solution)/shard_map/all_to_all | solution.py:11
  316.4 4.3 broadcast_in_dim.94
  320.6 5.7 %all-to-all-start.1 = ((bf16[4,32,128,256]{3,2,1,0:T(8,128)(2,1)}), bf16[4,32,128,256]{3,2,1,0:T(8,128)(2,1)}, u32[]{:S(2)}, u32[]{:S(2)}) async-start(bf16[4,32,128,256]{3,2,1,0:T(8,128)(2,1)} %broadcast_in_dim.94), calls=%async_computation.1 | async-start | bytes 16777216 | tf_op jit(solution)/shard_map/all_to_all | solution.py:11
  326.7 6.5 %fusion.18 = (f32[256]{0:T(256)S(1)}, bf16[256,1024]{1,0:T(8,128)(2,1)S(1)}) fusion(bf16[256,1024]{1,0:T(8,128)(2,1)S(1)} %copy-done, bf16[256,4096]{0,1:T(8,128)(2,1)} %bitcast.12, bf16[1024,4096]{1,0:T(8,128)(2,1)} %param.11), kind=kOutput, calls=%fused_computation.27 | convolution fusion | flops 2148794112 | bytes 11535360 | tf_op jit(solution)/shard_map/dot_general | solution.py:74
  333.2 86.0 %all-to-all-done.1 = bf16[4,32,128,256]{3,2,1,0:T(8,128)(2,1)} async-done(((bf16[4,32,128,256]{3,2,1,0:T(8,128)(2,1)}), bf16[4,32,128,256]{3,2,1,0:T(8,128)(2,1)}, u32[]{:S(2)}, u32[]{:S(2)}) %all-to-all-start.1) | async-done | bytes 8388640 | tf_op jit(solution)/shard_map/all_to_all | solution.py:11
  419.2 4.9 %convert_reduce_fusion = bf16[32,128,256]{2,1,0:T(8,128)(2,1)S(1)} fusion(bf16[4,32,128,256]{3,2,1,0:T(8,128)(2,1)} %all-to-all-done.1), kind=kLoop, calls=%fused_computation.6 | loop fusion | flops 7340032 | bytes 10485760 | tf_op jit(solution)/shard_map/reduce_sum | solution.py:15
  424.1 11.4 %convolution_convert_fusion = bf16[32,128,1024]{2,1,0:T(8,128)(2,1)} fusion(bf16[32,256,1024]{2,1,0:T(8,128)(2,1)} %all-gather.2.cloned.1.call-done, bf16[32,128,256]{2,1,0:T(8,128)(2,1)S(1)} %convert_reduce_fusion), kind=kOutput, calls=%fused_computation.11 | convolution fusion | flops 2154823680 | bytes 27262976 | tf_op jit(solution)/shard_map/ncb,nbd->ncd/dot_general | solution.py:92
  435.5 15.4 %gather_fusion.1 = bf16[2048,1024]{1,0:T(8,128)(2,1)} fusion(bf16[4096,1024]{1,0:T(8,128)(2,1)} %bitcast.56, s32[2048]{0:T(1024)S(1)} %broadcast_clamp_fusion), kind=kCustom, calls=%fused_computation.1 | custom fusion | bytes 8396800 | tf_op jit(solution)/shard_map/jit(_take)/gather | solution.py:98
  450.9 5.3 %fusion.9 = f32[256,1,8]{2,1,0:T(1,128)S(1)} fusion(bf16[2048,1024]{1,0:T(8,128)(2,1)} %gather_fusion.1, pred[256,8]{1,0:T(8,128)(4,1)S(1)} %copy.38, bf16[256,1024,1]{1,0,2:T(8,128)(2,1)S(1)} %bitcast.64), kind=kOutput, calls=%fused_computation.18 | convolution fusion | flops 6291456 | bytes 4728832 | tf_op jit(solution)/shard_map/rkd,rd->rk/dot_general | solution.py:104
  456.3 7.8 %all_to_all.26 = f32[4,256,8]{1,2,0:T(8,128)S(1)} all-to-all(f32[4,256,8]{1,2,0:T(8,128)S(1)} %broadcast_in_dim.98), channel_id=1, replica_groups=mesh['adapter'=32,'mp'=4] {'mp'}, dimensions={0} | all-to-all | bytes 65536 | tf_op jit(solution)/shard_map/all_to_all | solution.py:11
  464.3 5.8 %fusion.8 = f32[256,1,1024]{2,1,0:T(1,128)S(1)} fusion(f32[256,8,1]{1,2,0:T(1,128)S(1)} %copy.46, bf16[2048,1024]{1,0:T(8,128)(2,1)} %gather_fusion.1, pred[256,8]{1,0:T(8,128)(4,1)S(1)} %copy.38), kind=kOutput, calls=%fused_computation.17 | convolution fusion | flops 27262976 | bytes 5253120 | tf_op jit(solution)/shard_map/rk,rkd->rd/dot_general | solution.py:109
  470.1 1.1 fusion.19
  (41 shorter events, 2.9 us)
Async XLA Ops:
  6.5 417.6 %all-gather.2.cloned.1.call-start = ((), (), s32[]{:S(2)}) async-start(), calls=%async_computation.5 | async-start | bytes 17301504 | tf_op jit(solution)/shard_map/all_gather | solution.py:95
  13.2 31.6 %copy-start.1 = (bf16[1,1024,256]{2,1,0:T(8,128)(2,1)S(1)}, bf16[1,1024,256]{2,1,0:T(8,128)(2,1)}, u32[]{:S(2)}) copy-start(bf16[1,1024,256]{2,1,0:T(8,128)(2,1)} %param.8) | copy-start | bytes 1572868
  51.2 7.6 %copy-start.2 = (s32[256,8]{0,1:T(8,128)S(1)}, s32[256,8]{0,1:T(8,128)}, u32[]{:S(2)}) copy-start(s32[256,8]{0,1:T(8,128)} %param.7) | copy-start | bytes 24580
  51.3 232.1 %all-to-all-start = ((bf16[32,1,1024,256]{3,2,1,0:T(8,128)(2,1)}), bf16[32,1,1024,256]{3,2,1,0:T(8,128)(2,1)}, u32[]{:S(2)}, u32[]{:S(2)}) async-start(bf16[32,1,1024,256]{3,2,1,0:T(8,128)(2,1)} %stack.2), calls=%async_computation | async-start | bytes 33554432 | tf_op jit(solution)/shard_map/all_to_all | solution.py:83
  58.9 9.5 %copy-start = (bf16[256,1024]{1,0:T(8,128)(2,1)S(1)}, bf16[256,1024]{1,0:T(8,128)(2,1)}, u32[]{:S(2)}) copy-start(bf16[256,1024]{1,0:T(8,128)(2,1)} %param.6) | copy-start | bytes 1572868
  284.9 31.5 %all-to-all-start.3 = ((bf16[4,256,1024]{1,2,0:T(8,128)(2,1)}), bf16[4,256,1024]{1,2,0:T(8,128)(2,1)}, u32[]{:S(2)}, u32[]{:S(2)}) async-start(bf16[4,256,1024]{1,2,0:T(8,128)(2,1)} %broadcast_in_dim.97), calls=%async_computation.3 | async-start | bytes 4194304 | tf_op jit(solution)/shard_map/all_to_all | solution.py:11
  320.6 98.6 %all-to-all-start.1 = ((bf16[4,32,128,256]{3,2,1,0:T(8,128)(2,1)}), bf16[4,32,128,256]{3,2,1,0:T(8,128)(2,1)}, u32[]{:S(2)}, u32[]{:S(2)}) async-start(bf16[4,32,128,256]{3,2,1,0:T(8,128)(2,1)} %broadcast_in_dim.94), calls=%async_computation.1 | async-start | bytes 16777216 | tf_op jit(solution)/shard_map/all_to_all | solution.py:11
Sparse Core Ops, SparseCore 0:
  9.6 194.5 all-gather.1
